TPU v7x, 32 devices: a whole 2x2x4 slice. The times are simulated.
32 devices in a mesh: outer: 8 (over y, x, core), inner: 4 (over z).
Axes of the slice: x: 2, y: 2, z: 4, core: 2. Of those that a mesh axis runs over, the one named last changes fastest.
Arguments:
- leaf_fronts: float32 [32, 512, 512], P(('outer', 'inner')), as said below
- pivot_count: int32 [32], P(('outer', 'inner')), may hold values from 64 to 256, as said below
- update_rows: int32 [32, 256], P(('outer', 'inner')), may hold values from 0 to 8191, as said below
- top_front: float32 [8192, 8192], P('outer', 'inner'), as said below
Outputs:
- factor: float32 [8192, 128], P('outer')
- schur: float32 [8192, 8192], P('outer', 'inner')
Inputs may be any that keep to these rules, and one draw needn't show every extreme that they name: `pivot_count`: a multiple of 64; both ends occur. `update_rows`: each row strictly increases and holds exactly 32 entries in each block of 1024 consecutive top front rows. `leaf_fronts`: each front is symmetric positive definite. `top_front`: symmetric positive definite.
All inputs are finite; a program needn't handle non-finite values.
Results may differ from a plain program's by a relative error of at most 0.0003.
Values sent between devices are 32-bit elements; how exact they have to be, the bound alone decides.
A program may use at most 64 MiB of HBM per device.

v0:
```python
import functools

import jax
import jax.numpy as jnp
from jax import lax
from jax.experimental import pallas as pl
from jax.experimental.pallas import tpu as pltpu
from jax.sharding import PartitionSpec as P

PV = 256
U = 256
PIV = 128
NB = 64


def iota(shape, dim):
    return lax.broadcasted_iota(jnp.int32, shape, dim)


def dot(a, b, ca=1, cb=0):
    return lax.dot_general(
        a, b, (((ca,), (cb,)), ((), ())), preferred_element_type=jnp.float32
    )


def halves(x):
    high = x.astype(jnp.bfloat16)
    return high, (x - high.astype(jnp.float32)).astype(jnp.bfloat16)


def dot3(a, b, ca=1, cb=0):
    a_high, a_low = halves(a)
    b_high, b_low = halves(b)
    return dot(a_high, b_high, ca, cb) + (dot(a_high, b_low, ca, cb) + dot(a_low, b_high, ca, cb))


def dot6(a, b, ca=1, cb=0):
    return lax.dot_general(
        a,
        b,
        (((ca,), (cb,)), ((), ())),
        precision=lax.Precision.HIGHEST,
        preferred_element_type=jnp.float32,
    )


def inverse_cholesky(block):
    order = block.shape[0]
    unit = (iota((order, order), 0) == iota((order, order), 1)).astype(jnp.float32)
    joined = jnp.concatenate([block, unit], axis=1)
    width = joined.shape[1]
    count = order // 8
    rows = [joined[8 * b : 8 * b + 8] for b in range(count)]
    sub = iota((8, width), 0)
    scales = []
    for k in range(count):
        cols = {
            b: [
                jnp.broadcast_to(rows[b][:, 8 * k + j : 8 * k + j + 1], (8, width))
                for j in range(8)
            ]
            for b in range(k, count)
        }
        scale = jnp.zeros((8, width), jnp.float32)
        for j in range(8):
            pivot = jnp.broadcast_to(cols[k][j][j : j + 1], (8, width))
            inverse = 1.0 / pivot
            scale = jnp.where(sub == j, lax.rsqrt(pivot), scale)
            row = jnp.broadcast_to(rows[k][j : j + 1], (8, width))
            heads = [jnp.broadcast_to(cols[k][l][j : j + 1], (8, width)) for l in range(8)]
            for b in range(k, count):
                weight = cols[b][j] * inverse
                if b == k:
                    weight = jnp.where(sub > j, weight, 0.0)
                rows[b] = rows[b] - weight * row
                for l in range(j + 1, 8):
                    cols[b][l] = cols[b][l] - weight * heads[l]
        scales.append(scale)
    scaled = jnp.concatenate([rows[b] * scales[b] for b in range(count)], axis=0)
    return scaled[:, order:]


def leaf_kernel(
    n_outer,
    n_inner,
    pivots_ref,
    front_ref,
    index_ref,
    top_ref,
    panel_out,
    tile_out,
    index_out,
    slab_out,
    columns_out,
    pivot_out,
    work,
    panel_send,
    tile_send,
    slab,
    columns,
    pivot,
    send_sem,
    recv_sem,
    slab_send,
    slab_recv,
    columns_send,
    columns_recv,
    pivot_send,
    pivot_recv,
    local_sem,
):
    outer_index = lax.axis_index("outer")
    inner_index = lax.axis_index("inner")
    leaves = n_outer * n_inner
    flat = outer_index * n_inner + inner_index
    slab_parts, column_parts = slab_recv.shape[0], columns_recv.shape[0]
    slab_rows = slab.shape[0] // slab_parts
    column_rows = columns.shape[0] // column_parts

    def away(offset):
        target = lax.rem(flat + offset, leaves)
        return target, (lax.div(target, n_inner), lax.rem(target, n_inner))

    def remote(source, landing, sent, got, device):
        return pltpu.make_async_remote_copy(
            src_ref=source,
            dst_ref=landing,
            send_sem=sent,
            recv_sem=got,
            device_id=device,
            device_id_type=pl.DeviceIdType.MESH,
        )

    barrier = pltpu.get_barrier_semaphore()

    @pl.loop(1, leaves)
    def _(offset):
        pl.semaphore_signal(
            barrier, inc=1, device_id=away(offset)[1], device_id_type=pl.DeviceIdType.MESH
        )

    pl.semaphore_wait(barrier, leaves - 1)

    def slab_copy(gap, part):
        rows = pl.ds(part * slab_rows, slab_rows)
        level = slab_gaps.index(gap)
        device = (lax.rem(outer_index + gap, n_outer), inner_index)
        return remote(
            slab.at[rows], slab.at[rows], slab_send.at[level, part], slab_recv.at[part], device
        )

    def pivot_copy(gap):
        device = away(gap)[1]
        return remote(pivot, pivot, pivot_send.at[flat_gaps.index(gap)], pivot_recv, device)

    def column_copy(part):
        rows = pl.ds(part * column_rows, column_rows)
        device = (outer_index, lax.rem(inner_index + 1, n_inner))
        return remote(
            columns.at[rows], columns.at[rows], columns_send.at[part], columns_recv.at[part], device
        )

    def halvings(count):
        gaps = []
        while count > 1:
            count //= 2
            gaps.append(count)
        return gaps

    slab_gaps, flat_gaps = halvings(n_outer), halvings(leaves)

    def slab_relay(gap, part):
        @pl.when(lax.rem(outer_index, 2 * gap) == gap)
        def _():
            slab_copy(gap, part).wait_recv()
            for lower in slab_gaps:
                if lower < gap:
                    slab_copy(lower, part).start()

    def pivot_relay(gap):
        @pl.when(lax.rem(flat, 2 * gap) == gap)
        def _():
            pivot_copy(gap).wait_recv()
            for lower in flat_gaps:
                if lower < gap:
                    pivot_copy(lower).start()

    def column_relay(hop, part):
        @pl.when(inner_index == hop)
        def _():
            column_copy(part).wait_recv()
            if hop < n_inner - 1:
                column_copy(part).start()

    local_pivot = pltpu.make_async_copy(
        top_ref.at[pl.ds(0, PIV), pl.ds(0, PIV)], pivot, local_sem.at[0]
    )
    local_slab = pltpu.make_async_copy(top_ref.at[pl.ds(0, PIV), :], slab, local_sem.at[1])
    local_columns = pltpu.make_async_copy(top_ref.at[:, pl.ds(0, PIV)], columns, local_sem.at[2])

    @pl.when(flat == 0)
    def _():
        local_pivot.start()

    @pl.when(outer_index == 0)
    def _():
        local_slab.start()

    @pl.when(inner_index == 0)
    def _():
        local_columns.start()

    def index_copy(offset):
        target, device = away(offset)
        return remote(
            index_ref.at[target],
            index_out.at[flat],
            send_sem.at[2, offset],
            recv_sem.at[2, offset],
            device,
        )

    @pl.when(flat == 0)
    def _():
        local_pivot.wait()
        for gap in flat_gaps:
            pivot_copy(gap).start()

    @pl.when(outer_index == 0)
    def _():
        local_slab.wait()
        for part in range(slab_parts):
            for gap in slab_gaps:
                slab_copy(gap, part).start()

    @pl.when(inner_index == 0)
    def _():
        local_columns.wait()
        for part in range(column_parts):
            column_copy(part).start()

    @pl.loop(1, leaves)
    def _(offset):
        index_copy(offset).start()

    pending = [
        (lambda gap=gap: pivot_relay(gap), order + 1) for order, gap in enumerate(flat_gaps)
    ]
    for hop in range(1, n_inner):
        for part in range(column_parts):
            pending.append((lambda hop=hop, part=part: column_relay(hop, part), hop + part + 0.5))
    for order, gap in enumerate(slab_gaps):
        for part in range(slab_parts):
            pending.append(
                (lambda gap=gap, part=part: slab_relay(gap, part), 2 * order + 2 * part + 2.6)
            )
    pending.sort(key=lambda entry: entry[1])

    def relay(limit):
        while pending and pending[0][1] <= limit:
            pending.pop(0)[0]()

    live = pivots_ref[0]
    row = iota((PV, PV + U), 0)
    col = iota((PV, PV + U), 1)
    keep = (row < live) & ((col < live) | (col >= PV))
    unit = jnp.where((row == col) & (row >= live), 1.0, 0.0)
    work[...] = jnp.where(keep, front_ref[0, :PV, :], unit)
    for start in range(0, PV, NB):
        stop = start + NB
        inverse = inverse_cholesky(work[start:stop, start:stop])
        solved = dot6(inverse, work[start:stop, :])
        work[start:stop, :] = solved
        if stop < PV:
            work[stop:, :] = work[stop:, :] - dot6(solved[:, stop:PV], solved, 0, 0)
            relay(stop // NB)
    coupling = work[:, PV:]
    update = front_ref[0, PV:, PV:] - dot6(coupling, coupling, 0, 0)
    per_row, per_col = U // n_outer, U // n_inner
    half = per_row // 2
    lead = update[:per_row]
    for o in range(n_outer):
        for i in range(n_inner):
            chosen = slice(i * per_col, (i + 1) * per_col)
            panel_send[o * n_inner + i] = jnp.concatenate(
                [
                    lead[:, :per_row],
                    lead[:, chosen],
                    lead[:, o * per_row : (o + 1) * per_row],
                ],
                axis=1,
            )
            first = o * per_row
            tile_send[o * n_inner + i] = jnp.concatenate(
                [
                    update[first : first + half, chosen],
                    update[first + half : first + per_row, chosen],
                ],
                axis=1,
            )

    def panel_copy(offset):
        target, device = away(offset)
        return remote(
            panel_send.at[target],
            panel_out.at[flat],
            send_sem.at[0, offset],
            recv_sem.at[0, offset],
            device,
        )

    def tile_copy(offset):
        target, device = away(offset)
        return remote(
            tile_send.at[target],
            tile_out.at[flat],
            send_sem.at[1, offset],
            recv_sem.at[1, offset],
            device,
        )

    @pl.loop(1, leaves)
    def _(offset):
        panel_copy(offset).start()

    @pl.loop(1, leaves)
    def _(offset):
        tile_copy(offset).start()

    own = [
        pltpu.make_async_copy(panel_send.at[flat], panel_out.at[flat], local_sem.at[3]),
        pltpu.make_async_copy(tile_send.at[flat], tile_out.at[flat], local_sem.at[4]),
        pltpu.make_async_copy(index_ref.at[flat], index_out.at[flat], local_sem.at[5]),
    ]
    for copy in own:
        copy.start()
    relay(1 << 20)
    own.append(pltpu.make_async_copy(slab, slab_out, local_sem.at[6]))
    own.append(pltpu.make_async_copy(columns, columns_out, local_sem.at[7]))
    own.append(pltpu.make_async_copy(pivot, pivot_out, local_sem.at[8]))
    for copy in own[3:]:
        copy.start()

    @pl.loop(1, leaves)
    def _(offset):
        index_copy(offset).wait()
        panel_copy(offset).wait()
        tile_copy(offset).wait()

    for level, gap in enumerate(slab_gaps):
        @pl.when(lax.rem(outer_index, 2 * gap) == 0)
        def _():
            for part in range(slab_parts):
                slab_copy(gap, part).wait_send()

    for gap in flat_gaps:
        @pl.when(lax.rem(flat, 2 * gap) == 0)
        def _():
            pivot_copy(gap).wait_send()

    @pl.when(inner_index < n_inner - 1)
    def _():
        for part in range(column_parts):
            column_copy(part).wait_send()

    for copy in own:
        copy.wait()


def panel_kernel(
    shape,
    panel_ref,
    index_ref,
    pivot_ref,
    slab_ref,
    columns_ref,
    factor_ref,
    slab_factor_ref,
    e_pivot,
    e_slab,
    e_row,
    lead_sub,
    row_sub,
    col_sub,
):
    leaves, per_row, per_col, tile_rows, tile_cols = shape
    turned = index_ref[...].astype(jnp.float32).T.astype(jnp.int32)
    for d in range(leaves):
        lanes = index_ref[d : d + 1, :per_row]
        lead_sub[d * per_row : (d + 1) * per_row, :] = turned[:per_row, d : d + 1]
        col_sub[d * per_col : (d + 1) * per_col, :] = turned[per_row : per_row + per_col, d : d + 1]
        row_sub[d * per_row : (d + 1) * per_row, :] = turned[per_row + per_col :, d : d + 1]
        pick = (iota((PIV, per_row), 0) == lanes).astype(jnp.bfloat16)
        high, low = halves(panel_ref[d])
        spread = dot(pick, high) + dot(pick, low)
        e_pivot[:, d * per_row : (d + 1) * per_row] = spread[:, :per_row]
        e_slab[:, d * per_col : (d + 1) * per_col] = spread[:, per_row : per_row + per_col]
        e_row[:, d * per_row : (d + 1) * per_row] = spread[:, per_row + per_col :]

    def place(source, index_ref, width):
        depth = source.shape[1]
        pick = (iota((depth, width), 1) == index_ref[...]).astype(jnp.bfloat16)
        high, low = halves(source)
        return dot(high, pick) + dot(low, pick)

    pivot = pivot_ref[...] + place(e_pivot[...], lead_sub, PIV)
    first = inverse_cholesky(pivot[:NB, :NB])
    across = dot6(first, pivot[:NB, NB:])
    second = inverse_cholesky(pivot[NB:, NB:] - dot6(across, across, 0, 0))
    below = -dot6(second, dot6(across, first, 0, 0))
    inverse = jnp.concatenate(
        [
            jnp.concatenate([first, jnp.zeros_like(first)], axis=1),
            jnp.concatenate([below, second], axis=1),
        ],
        axis=0,
    )
    width = min(tile_cols, 512)
    for start in range(0, tile_cols, width):
        pick = (iota((leaves * per_col, width), 1) + start == col_sub[...]).astype(jnp.bfloat16)
        high, low = halves(e_slab[...])
        part = slab_ref[:, start : start + width] + (dot(high, pick) + dot(low, pick))
        slab_factor_ref[:, start : start + width] = dot3(inverse, part)
    width = min(tile_rows, 512)
    for start in range(0, tile_rows, width):
        pick = (iota((leaves * per_row, width), 1) + start == row_sub[...]).astype(jnp.bfloat16)
        high, low = halves(e_row[...])
        part = columns_ref[start : start + width, :].T + (dot(high, pick) + dot(low, pick))
        factor_ref[start : start + width, :] = dot3(inverse, part).T

    outer_index = lax.axis_index("outer")

    @pl.when(outer_index * tile_rows < PIV)
    def _():
        for start in range(0, tile_rows, 128):
            span = min(128, tile_rows - start)
            rows = outer_index * tile_rows + start + iota((span, PIV), 0)
            block = factor_ref[start : start + span, :]
            factor_ref[start : start + span, :] = jnp.where(
                rows >= iota((span, PIV), 1), block, 0.0
            )


def trailing_kernel(
    shape,
    tile_ref,
    index_ref,
    top_ref,
    factor_ref,
    slab_ref,
    schur_ref,
    high_ref,
    low_ref,
    row_lane,
):
    leaves, per_row, per_col, tile_rows, tile_cols = shape
    step = pl.program_id(0)
    height = top_ref.shape[0]
    half = per_row // 2

    @pl.when(step == 0)
    def _():
        turned = index_ref[...].astype(jnp.float32).T.astype(jnp.int32)
        for d in range(leaves):
            row_lane[:, d * per_row : (d + 1) * per_row] = index_ref[
                d : d + 1, per_row + per_col :
            ]
            packed = tile_ref[d]
            values = jnp.concatenate([packed[:, :per_col], packed[:, per_col:]], axis=0)
            pick = (
                iota((per_col, tile_cols), 1) == turned[per_row : per_row + per_col, d : d + 1]
            ).astype(jnp.bfloat16)
            high, low = halves(values)
            spread = dot(high, pick)
            spread_low = dot(low, pick)
            high_ref[d * per_row : (d + 1) * per_row, :] = spread.astype(jnp.bfloat16)
            low_ref[d * per_row : (d + 1) * per_row, :] = spread_low.astype(jnp.bfloat16)

    rows = step * height + iota((height, leaves * per_row), 0)
    pick = (rows == row_lane[...]).astype(jnp.bfloat16)
    f_high, f_low = halves(-factor_ref[...])
    width = min(tile_cols, 512)
    row_global = lax.axis_index("outer") * tile_rows + step * height + iota((height, width), 0)
    for start in range(0, tile_cols, width):
        cols = slice(start, start + width)
        s_high, s_low = halves(slab_ref[:, cols])
        total = dot(pick, high_ref[:, cols]) + dot(pick, low_ref[:, cols])
        total = total + (dot(f_high, s_high) + (dot(f_high, s_low) + dot(f_low, s_high)))
        col_global = lax.axis_index("inner") * tile_cols + start + iota((height, width), 1)
        keep = (row_global >= PIV) & (col_global >= PIV)
        schur_ref[:, cols] = jnp.where(keep, top_ref[:, cols] + total, 0.0)


def shards(leaf_fronts, pivot_count, update_rows, top_front):
    n_outer = lax.axis_size("outer")
    n_inner = lax.axis_size("inner")
    tile_rows, tile_cols = top_front.shape
    leaves = n_outer * n_inner
    per_row, per_col = U // n_outer, U // n_inner
    shape = (leaves, per_row, per_col, tile_rows, tile_cols)
    vmem = pl.BlockSpec(memory_space=pltpu.VMEM)
    big = pltpu.CompilerParams(vmem_limit_bytes=56 << 20)

    lead = update_rows[0, :per_row]
    rows = (update_rows[0] % tile_rows).reshape(n_outer, 1, per_row)
    cols = (update_rows[0] % tile_cols).reshape(1, n_inner, per_col)
    grid = (n_outer, n_inner)
    messages = jnp.concatenate(
        [
            jnp.broadcast_to(lead, grid + (per_row,)),
            jnp.broadcast_to(cols, grid + (per_col,)),
            jnp.broadcast_to(rows, grid + (per_row,)),
        ],
        axis=2,
    )
    lanes = 2 * per_row + per_col
    messages = messages.reshape(leaves, 1, lanes)

    levels = (n_outer - 1).bit_length()
    slab_parts, column_parts = 2, 4
    anywhere = pl.BlockSpec(memory_space=pl.ANY)
    dma = pltpu.SemaphoreType.DMA
    real = lambda *dims: jax.ShapeDtypeStruct(dims, jnp.float32)
    panel, tiles, indices, slab, columns, pivot_raw = pl.pallas_call(
        functools.partial(leaf_kernel, n_outer, n_inner),
        out_shape=(
            real(leaves, per_row, lanes),
            real(leaves, per_row // 2, 2 * per_col),
            jax.ShapeDtypeStruct((leaves, 1, lanes), jnp.int32),
            real(PIV, tile_cols),
            real(tile_rows, PIV),
            real(PIV, PIV),
        ),
        in_specs=[pl.BlockSpec(memory_space=pltpu.SMEM), vmem, vmem, anywhere],
        out_specs=(anywhere,) * 6,
        scratch_shapes=[
            pltpu.VMEM((PV, PV + U), jnp.float32),
            pltpu.VMEM((leaves, per_row, lanes), jnp.float32),
            pltpu.VMEM((leaves, per_row // 2, 2 * per_col), jnp.float32),
            pltpu.VMEM((PIV, tile_cols), jnp.float32),
            pltpu.VMEM((tile_rows, PIV), jnp.float32),
            pltpu.VMEM((PIV, PIV), jnp.float32),
            dma((3, leaves)),
            dma((3, leaves)),
            dma((levels, slab_parts)),
            dma((slab_parts,)),
            dma((column_parts,)),
            dma((column_parts,)),
            dma(((leaves - 1).bit_length(),)),
            dma,
            dma((9,)),
        ],
        compiler_params=pltpu.CompilerParams(
            vmem_limit_bytes=56 << 20, collective_id=0, has_side_effects=True
        ),
    )(pivot_count, leaf_fronts, messages, top_front)
    indices = indices.reshape(leaves, lanes)

    factor, slab_factor = pl.pallas_call(
        functools.partial(panel_kernel, shape),
        out_shape=(real(tile_rows, PIV), real(PIV, tile_cols)),
        in_specs=[vmem] * 5,
        out_specs=(vmem, vmem),
        scratch_shapes=[
            pltpu.VMEM((PIV, leaves * per_row), jnp.float32),
            pltpu.VMEM((PIV, leaves * per_col), jnp.float32),
            pltpu.VMEM((PIV, leaves * per_row), jnp.float32),
            pltpu.VMEM((leaves * per_row, 1), jnp.int32),
            pltpu.VMEM((leaves * per_row, 1), jnp.int32),
            pltpu.VMEM((leaves * per_col, 1), jnp.int32),
        ],
        compiler_params=big,
    )(panel, indices, pivot_raw, slab, columns)

    height = min(tile_rows, 128)
    whole = lambda *dims: pl.BlockSpec(dims, lambda r: (0,) * len(dims))
    schur = pl.pallas_call(
        functools.partial(trailing_kernel, shape),
        out_shape=jax.ShapeDtypeStruct((tile_rows, tile_cols), jnp.float32),
        grid=(tile_rows // height,),
        in_specs=[
            whole(leaves, per_row // 2, 2 * per_col),
            whole(leaves, lanes),
            pl.BlockSpec((height, tile_cols), lambda r: (r, 0)),
            pl.BlockSpec((height, PIV), lambda r: (r, 0)),
            whole(PIV, tile_cols),
        ],
        out_specs=pl.BlockSpec((height, tile_cols), lambda r: (r, 0)),
        scratch_shapes=[
            pltpu.VMEM((leaves * per_row, tile_cols), jnp.bfloat16),
            pltpu.VMEM((leaves * per_row, tile_cols), jnp.bfloat16),
            pltpu.VMEM((1, leaves * per_row), jnp.int32),
        ],
        compiler_params=big,
    )(tiles, indices, top_front, factor, slab_factor)
    return (factor, schur)


def solution(mesh):
    placed = (
        P(("outer", "inner"), None, None),
        P(("outer", "inner")),
        P(("outer", "inner"), None),
        P("outer", "inner"),
    )
    return jax.shard_map(
        shards,
        mesh=mesh,
        in_specs=placed,
        out_specs=(P("outer", None), P("outer", "inner")),
        check_vma=False,
    )
```

profile of v0, /device:TPU:23, one launch (start us, length us, event | category | flops | bytes accessed | tf_op | source)
XLA Modules:
  0.0 93.0 jit_solution(17580242519155198445)
XLA Ops:
  1.3 0.5 broadcast.60
  1.8 1.3 %reduce.5 = s32[256]{0:T(256)S(1)} reduce(s32[1,256]{1,0:T(1,128)} %param.6, s32[]{:T(128)} %broadcast.60), dimensions={0}, to_apply=%param.6.reduce_sub_computation.5 | reduce | bytes 2052 | tf_op args[2]
  3.1 0.7 slice_bitcast_fusion
  3.8 0.1 squeeze.10
  3.9 0.8 squeeze.11
  4.7 0.7 pad_add_fusion
  5.4 53.3 %shard_map.59 = (f32[32,32,128]{2,1,0:T(8,128)}, f32[32,16,128]{2,1,0:T(8,128)}, s32[32,1,128]{2,1,0:T(1,128)}, f32[128,2048]{1,0:T(8,128)}, f32[1024,128]{1,0:T(8,128)}, /*index=5*/f32[128,128]{1,0:T(8,128)}) custom-call(s32[1]{0:T(128)S(6)} %copy.6.pivots_ref, f32[1,512,512]{2,1,0:T(8,128)} %front_ref.1, s32[32,1,128]{2,1,0:T(1,128)} %bitcast.5, ...), custom_call_target="tpu_custom_call" | custom-call | tf_op jit(solution)/shard_map/pallas_call | solution.py:524
  58.7 14.0 %shard_map.60 = (f32[1024,128]{1,0:T(8,128)}, f32[128,2048]{1,0:T(8,128)}) custom-call(f32[32,32,128]{2,1,0:T(8,128)} %get-tuple-element.10.panel_ref, s32[32,128]{1,0:T(8,128)} %bitcast.6, f32[128,128]{1,0:T(8,128)} %get-tuple-element.12.pivot_ref, f32[128,2048]{1,0:T(8,128)} %get-tuple-element.13.slab_ref, f32[1024,128]{1,0:T(8,128)} %get-tuple-element.14.columns_ref), custom_call_target="tpu_custom_call" | custom-call | tf_op jit(solution)/shard_map/pallas_call | solution.py:559
  72.7 20.3 %shard_map.61 = f32[1024,2048]{1,0:T(8,128)} custom-call(f32[32,16,128]{2,1,0:T(8,128)} %get-tuple-element.16.tile_ref, s32[32,128]{1,0:T(8,128)} %bitcast.7, f32[1024,2048]{1,0:T(8,128)} %top_ref.3, f32[1024,128]{1,0:T(8,128)} %get-tuple-element.8.factor_ref, f32[128,2048]{1,0:T(8,128)} %get-tuple-element.17.slab_ref), custom_call_target="tpu_custom_call" | custom-call | tf_op jit(solution)/shard_map/pallas_call | solution.py:577
  (5 shorter events, 0.0 us)
where the time goes:
time: 93.3 us; the launch traced here: 93 us
  Pallas kernels  87.6 us (94%)
  other arithmetic  2.06 us (2%)
  local copies, waits for them, and re-layouts  2.02 us (2%)
  between operations  1.29 us (1%)
    pallas_call x1, Pallas kernels, shards(): pl.pallas_call(functools.partial(leaf_kernel, n_outer, n_inner), out_shap...  53.3 us
    pallas_call x1, Pallas kernels, shards(): pl.pallas_call(functools.partial(trailing_kernel, shape), out_shape=jax.S...  20.3 us
    pallas_call x1, Pallas kernels, shards(): pl.pallas_call(functools.partial(panel_kernel, shape), out_shape=(real(ti...  14 us

commit v1 on v0

--- a/solution.py
+++ b/solution.py
@@ -88,14 +88,14 @@
     index_ref,
     top_ref,
     panel_out,
-    tile_out,
+    tile_ref,
     index_out,
     slab_out,
     columns_out,
     pivot_out,
     work,
     panel_send,
-    tile_send,
+    index_send,
     slab,
     columns,
     pivot,
@@ -213,10 +213,10 @@
     def index_copy(offset):
         target, device = away(offset)
         return remote(
-            index_ref.at[target],
+            index_send.at[target],
             index_out.at[flat],
-            send_sem.at[2, offset],
-            recv_sem.at[2, offset],
+            send_sem.at[1, offset],
+            recv_sem.at[1, offset],
             device,
         )
 
@@ -238,6 +238,20 @@
         local_columns.wait()
         for part in range(column_parts):
             column_copy(part).start()
+
+    per_row, per_col = U // n_outer, U // n_inner
+    tile_rows, tile_cols = top_ref.shape
+    targets = index_ref[...]
+    for o in range(n_outer):
+        for i in range(n_inner):
+            index_send[o * n_inner + i] = jnp.concatenate(
+                [
+                    targets[:, :per_row],
+                    targets[:, i * per_col : (i + 1) * per_col] - i * tile_cols,
+                    targets[:, o * per_row : (o + 1) * per_row] - o * tile_rows,
+                ],
+                axis=1,
+            )
 
     @pl.loop(1, leaves)
     def _(offset):
@@ -276,7 +290,6 @@
             relay(stop // NB)
     coupling = work[:, PV:]
     update = front_ref[0, PV:, PV:] - dot6(coupling, coupling, 0, 0)
-    per_row, per_col = U // n_outer, U // n_inner
     half = per_row // 2
     lead = update[:per_row]
     for o in range(n_outer):
@@ -291,7 +304,7 @@
                 axis=1,
             )
             first = o * per_row
-            tile_send[o * n_inner + i] = jnp.concatenate(
+            tile_ref[o * n_inner + i] = jnp.concatenate(
                 [
                     update[first : first + half, chosen],
                     update[first + half : first + per_row, chosen],
@@ -309,43 +322,29 @@
             device,
         )
 
-    def tile_copy(offset):
-        target, device = away(offset)
-        return remote(
-            tile_send.at[target],
-            tile_out.at[flat],
-            send_sem.at[1, offset],
-            recv_sem.at[1, offset],
-            device,
-        )
+    relay(4)
 
     @pl.loop(1, leaves)
     def _(offset):
         panel_copy(offset).start()
 
-    @pl.loop(1, leaves)
-    def _(offset):
-        tile_copy(offset).start()
-
     own = [
         pltpu.make_async_copy(panel_send.at[flat], panel_out.at[flat], local_sem.at[3]),
-        pltpu.make_async_copy(tile_send.at[flat], tile_out.at[flat], local_sem.at[4]),
-        pltpu.make_async_copy(index_ref.at[flat], index_out.at[flat], local_sem.at[5]),
+        pltpu.make_async_copy(index_send.at[flat], index_out.at[flat], local_sem.at[4]),
     ]
     for copy in own:
         copy.start()
     relay(1 << 20)
-    own.append(pltpu.make_async_copy(slab, slab_out, local_sem.at[6]))
-    own.append(pltpu.make_async_copy(columns, columns_out, local_sem.at[7]))
-    own.append(pltpu.make_async_copy(pivot, pivot_out, local_sem.at[8]))
-    for copy in own[3:]:
+    own.append(pltpu.make_async_copy(slab, slab_out, local_sem.at[5]))
+    own.append(pltpu.make_async_copy(columns, columns_out, local_sem.at[6]))
+    own.append(pltpu.make_async_copy(pivot, pivot_out, local_sem.at[7]))
+    for copy in own[2:]:
         copy.start()
 
     @pl.loop(1, leaves)
     def _(offset):
         index_copy(offset).wait()
         panel_copy(offset).wait()
-        tile_copy(offset).wait()
 
     for level, gap in enumerate(slab_gaps):
         @pl.when(lax.rem(outer_index, 2 * gap) == 0)
@@ -369,21 +368,55 @@
 
 def panel_kernel(
     shape,
+    n_inner,
     panel_ref,
     index_ref,
     pivot_ref,
     slab_ref,
     columns_ref,
+    tile_ref,
     factor_ref,
     slab_factor_ref,
+    tile_out,
     e_pivot,
     e_slab,
     e_row,
     lead_sub,
     row_sub,
     col_sub,
+    send_sem,
+    recv_sem,
+    local_sem,
 ):
     leaves, per_row, per_col, tile_rows, tile_cols = shape
+    outer_index = lax.axis_index("outer")
+    flat = outer_index * n_inner + lax.axis_index("inner")
+
+    def away(offset):
+        target = lax.rem(flat + offset, leaves)
+        return target, (lax.div(target, n_inner), lax.rem(target, n_inner))
+
+    def tile_copy(offset):
+        target, device = away(offset)
+        return pltpu.make_async_remote_copy(
+            src_ref=tile_ref.at[target],
+            dst_ref=tile_out.at[flat],
+            send_sem=send_sem.at[offset],
+            recv_sem=recv_sem.at[offset],
+            device_id=device,
+            device_id_type=pl.DeviceIdType.MESH,
+        )
+
+    barrier = pltpu.get_barrier_semaphore()
+
+    @pl.loop(1, leaves)
+    def _(offset):
+        pl.semaphore_signal(
+            barrier, inc=1, device_id=away(offset)[1], device_id_type=pl.DeviceIdType.MESH
+        )
+
+    own = pltpu.make_async_copy(tile_ref.at[flat], tile_out.at[flat], local_sem)
+    own.start()
     turned = index_ref[...].astype(jnp.float32).T.astype(jnp.int32)
     for d in range(leaves):
         lanes = index_ref[d : d + 1, :per_row]
@@ -415,6 +448,12 @@
         ],
         axis=0,
     )
+    pl.semaphore_wait(barrier, leaves - 1)
+
+    @pl.loop(1, leaves)
+    def _(offset):
+        tile_copy(offset).start()
+
     width = min(tile_cols, 512)
     for start in range(0, tile_cols, width):
         pick = (iota((leaves * per_col, width), 1) + start == col_sub[...]).astype(jnp.bfloat16)
@@ -428,8 +467,6 @@
         part = columns_ref[start : start + width, :].T + (dot(high, pick) + dot(low, pick))
         factor_ref[start : start + width, :] = dot3(inverse, part).T
 
-    outer_index = lax.axis_index("outer")
-
     @pl.when(outer_index * tile_rows < PIV)
     def _():
         for start in range(0, tile_rows, 128):
@@ -439,6 +476,12 @@
             factor_ref[start : start + span, :] = jnp.where(
                 rows >= iota((span, PIV), 1), block, 0.0
             )
+
+    @pl.loop(1, leaves)
+    def _(offset):
+        tile_copy(offset).wait()
+
+    own.wait()
 
 
 def trailing_kernel(
@@ -501,20 +544,7 @@
     vmem = pl.BlockSpec(memory_space=pltpu.VMEM)
     big = pltpu.CompilerParams(vmem_limit_bytes=56 << 20)
 
-    lead = update_rows[0, :per_row]
-    rows = (update_rows[0] % tile_rows).reshape(n_outer, 1, per_row)
-    cols = (update_rows[0] % tile_cols).reshape(1, n_inner, per_col)
-    grid = (n_outer, n_inner)
-    messages = jnp.concatenate(
-        [
-            jnp.broadcast_to(lead, grid + (per_row,)),
-            jnp.broadcast_to(cols, grid + (per_col,)),
-            jnp.broadcast_to(rows, grid + (per_row,)),
-        ],
-        axis=2,
-    )
     lanes = 2 * per_row + per_col
-    messages = messages.reshape(leaves, 1, lanes)
 
     levels = (n_outer - 1).bit_length()
     slab_parts, column_parts = 2, 4
@@ -532,35 +562,39 @@
             real(PIV, PIV),
         ),
         in_specs=[pl.BlockSpec(memory_space=pltpu.SMEM), vmem, vmem, anywhere],
-        out_specs=(anywhere,) * 6,
+        out_specs=(anywhere, vmem) + (anywhere,) * 4,
         scratch_shapes=[
             pltpu.VMEM((PV, PV + U), jnp.float32),
             pltpu.VMEM((leaves, per_row, lanes), jnp.float32),
-            pltpu.VMEM((leaves, per_row // 2, 2 * per_col), jnp.float32),
+            pltpu.VMEM((leaves, 1, lanes), jnp.int32),
             pltpu.VMEM((PIV, tile_cols), jnp.float32),
             pltpu.VMEM((tile_rows, PIV), jnp.float32),
             pltpu.VMEM((PIV, PIV), jnp.float32),
-            dma((3, leaves)),
-            dma((3, leaves)),
+            dma((2, leaves)),
+            dma((2, leaves)),
             dma((levels, slab_parts)),
             dma((slab_parts,)),
             dma((column_parts,)),
             dma((column_parts,)),
             dma(((leaves - 1).bit_length(),)),
             dma,
-            dma((9,)),
+            dma((8,)),
         ],
         compiler_params=pltpu.CompilerParams(
             vmem_limit_bytes=56 << 20, collective_id=0, has_side_effects=True
         ),
-    )(pivot_count, leaf_fronts, messages, top_front)
+    )(pivot_count, leaf_fronts, update_rows, top_front)
     indices = indices.reshape(leaves, lanes)
 
-    factor, slab_factor = pl.pallas_call(
-        functools.partial(panel_kernel, shape),
-        out_shape=(real(tile_rows, PIV), real(PIV, tile_cols)),
-        in_specs=[vmem] * 5,
-        out_specs=(vmem, vmem),
+    factor, slab_factor, tiles = pl.pallas_call(
+        functools.partial(panel_kernel, shape, n_inner),
+        out_shape=(
+            real(tile_rows, PIV),
+            real(PIV, tile_cols),
+            real(leaves, per_row // 2, 2 * per_col),
+        ),
+        in_specs=[vmem] * 5 + [anywhere],
+        out_specs=(vmem, vmem, anywhere),
         scratch_shapes=[
             pltpu.VMEM((PIV, leaves * per_row), jnp.float32),
             pltpu.VMEM((PIV, leaves * per_col), jnp.float32),
@@ -568,11 +602,16 @@
             pltpu.VMEM((leaves * per_row, 1), jnp.int32),
             pltpu.VMEM((leaves * per_row, 1), jnp.int32),
             pltpu.VMEM((leaves * per_col, 1), jnp.int32),
+            dma((leaves,)),
+            dma((leaves,)),
+            dma,
         ],
-        compiler_params=big,
-    )(panel, indices, pivot_raw, slab, columns)
-
-    height = min(tile_rows, 128)
+        compiler_params=pltpu.CompilerParams(
+            vmem_limit_bytes=56 << 20, collective_id=1, has_side_effects=True
+        ),
+    )(panel, indices, pivot_raw, slab, columns, tiles)
+
+    height = min(tile_rows, 256)
     whole = lambda *dims: pl.BlockSpec(dims, lambda r: (0,) * len(dims))
     schur = pl.pallas_call(
         functools.partial(trailing_kernel, shape),

time: 93.3 us -> 86.1 us (0.923)
  the two profiles are of different devices: /device:TPU:23 before, /device:TPU:0 now
where the time goes in v1:
time: 86.1 us; the launch traced here: 85.9 us
  Pallas kernels  83.8 us (97%)
  between operations  1.3 us (2%)
    pallas_call x1, Pallas kernels, shards(): pl.pallas_call(functools.partial(leaf_kernel, n_outer, n_inner), out_shap...  37.3 us
    pallas_call x1, Pallas kernels, shards(): pl.pallas_call(functools.partial(panel_kernel, shape, n_inner), out_shape...  26.6 us
    pallas_call x1, Pallas kernels, shards(): pl.pallas_call(functools.partial(trailing_kernel, shape), out_shape=jax.S...  20 us

profile of v1, /device:TPU:0, one launch (start us, length us, event | category | flops | bytes accessed | tf_op | source)
XLA Modules:
  0.0 85.9 jit_solution(5495789738107021028)
XLA Ops:
  1.3 37.3 %shard_map.59 = (f32[32,32,128]{2,1,0:T(8,128)}, f32[32,16,128]{2,1,0:T(8,128)}, s32[32,1,128]{2,1,0:T(1,128)}, f32[128,2048]{1,0:T(8,128)}, f32[1024,128]{1,0:T(8,128)}, /*index=5*/f32[128,128]{1,0:T(8,128)}) custom-call(s32[1]{0:T(128)S(6)} %copy.7.pivots_ref, f32[1,512,512]{2,1,0:T(8,128)} %front_ref.1, s32[1,256]{1,0:T(1,128)} %index_ref.1, ...), custom_call_target="tpu_custom_call" | custom-call | tf_op jit(solution)/shard_map/pallas_call | solution.py:554
  38.5 26.6 %shard_map.60 = (f32[1024,128]{1,0:T(8,128)}, f32[128,2048]{1,0:T(8,128)}, f32[32,16,128]{2,1,0:T(8,128)}) custom-call(f32[32,32,128]{2,1,0:T(8,128)} %get-tuple-element.11.panel_ref, s32[32,128]{1,0:T(8,128)} %bitcast.1, f32[128,128]{1,0:T(8,128)} %get-tuple-element.13.pivot_ref, f32[128,2048]{1,0:T(8,128)} %get-tuple-element.14.slab_ref, ...), custom_call_target="tpu_custom_call" | custom-call | tf_op jit(solution)/shard_map/pallas_call | solution.py:589
  65.1 0.0 copy-start
  65.1 20.0 %shard_map.61 = f32[1024,2048]{1,0:T(8,128)} custom-call(f32[32,16,128]{2,1,0:T(8,128)} %get-tuple-element.18.tile_ref, s32[32,128]{1,0:T(8,128)} %bitcast.2, f32[1024,2048]{1,0:T(8,128)} %top_ref.3, f32[1024,128]{1,0:T(8,128)} %get-tuple-element.22.factor_ref, f32[128,2048]{1,0:T(8,128)} %get-tuple-element.19.slab_ref), custom_call_target="tpu_custom_call" | custom-call | tf_op jit(solution)/shard_map/pallas_call | solution.py:616
  85.1 0.0 copy-done
  85.1 0.8 copy.8
Async XLA Ops:
  65.1 20.0 %copy-start = (f32[1024,128]{1,0:T(8,128)S(1)}, f32[1024,128]{1,0:T(8,128)}, u32[]{:S(2)}) copy-start(f32[1024,128]{1,0:T(8,128)} %get-tuple-element.22.factor_ref) | copy-start | bytes 1572868
